TPU v7x, 32 devices: a whole 2x2x4 slice. The times are simulated.
32 devices in a mesh: row: 4 (over y, x), col: 8 (over z, core).
Axes of the slice: x: 2, y: 2, z: 4, core: 2. Of those that a mesh axis runs over, the one named last changes fastest.
Arguments:
- trailing_grad: bfloat16 [4, 8, 768, 24576], P(None, 'col', None, 'row'), may hold values from -6 to 6
- panel: bfloat16 [24576, 512], P(('row', 'col')), may hold values from -0.0390625 to 0.0390625
- panel_grad: float32 [24576, 512], P(('row', 'col')), may hold values from -6 to 6
- diag_factor: float32 [512, 512], replicated, may hold values from -2 to 2, as said below
- diag_grad: float32 [512, 512], replicated, may hold values from -6 to 6
Outputs:
- panel_adj: float32 [24576, 512], P(('row', 'col'))
- diag_adj: float32 [512, 512], replicated
Inputs may be any that keep to these rules, and one draw needn't show every extreme that they name: `diag_factor`: lower triangular with zeros above the diagonal; diagonal entries between 1 and 2.
All inputs are finite; a program needn't handle non-finite values.
Results may differ from a plain program's by a relative error of at most 0.0003.
Values may be sent and summed in bfloat16 or wider, within the bound.
A program may use at most 128 MiB of HBM per device.

v0:
```python
import jax
import jax.numpy as jnp
from jax import lax
from jax.sharding import PartitionSpec as P


def halve_lower(matrix):
    rows = lax.broadcasted_iota(jnp.int32, matrix.shape, 0)
    cols = lax.broadcasted_iota(jnp.int32, matrix.shape, 1)
    keep = jnp.where(rows > cols, 1.0, jnp.where(rows == cols, 0.5, 0.0)).astype(jnp.float32)
    return matrix * keep


def keep_lower(matrix):
    rows = lax.broadcasted_iota(jnp.int32, matrix.shape, 0)
    cols = lax.broadcasted_iota(jnp.int32, matrix.shape, 1)
    return jnp.where(rows >= cols, matrix, 0.0)


def right_solve(left, lower):
    right = jax.scipy.linalg.solve_triangular(lower, left.T, lower=True, trans=1).T
    return 0.5 * (right + right.T)


def on_device(trailing_grad, panel, panel_grad, diag_factor, diag_grad):
    local_flip = trailing_grad.reshape(-1, trailing_grad.shape[3])
    lower = jnp.tril(diag_factor)
    col_panel = lax.all_gather(panel, "row", axis=0, tiled=True)
    row_panel = lax.all_gather(panel, "col", axis=0, tiled=True)
    block = local_flip
    direct = lax.psum_scatter(
        lax.dot_general(
            block, col_panel, (((0,), (0,)), ((), ())), preferred_element_type=jnp.float32
        ),
        "col",
        scatter_dimension=0,
        tiled=True,
    )
    block = local_flip
    transposed = lax.psum_scatter(
        jnp.dot(block, row_panel, preferred_element_type=jnp.float32),
        "row",
        scatter_dimension=0,
        tiled=True,
    )
    reduced = panel_grad - direct - transposed
    panel_adj = jax.scipy.linalg.solve_triangular(lower, reduced.T, lower=True, trans=1).T
    contrib = lax.dot_general(
        panel_adj,
        panel.astype(jnp.float32),
        (((0,), (0,)), ((), ())),
        precision=lax.Precision.HIGHEST,
    )
    diag_new = diag_grad - lax.psum(contrib, ("row", "col"))
    inner = halve_lower(jnp.dot(lower.T, keep_lower(diag_new), precision=lax.Precision.HIGHEST))
    left = jax.scipy.linalg.solve_triangular(lower, inner, lower=True, trans=1)
    return (panel_adj, right_solve(left, lower))


def solution(mesh):
    in_specs = (
        P(None, "col", None, "row"),
        P(("row", "col"), None),
        P(("row", "col"), None),
        P(),
        P(),
    )
    out_specs = (P(("row", "col"), None), P())
    return jax.shard_map(
        on_device, mesh=mesh, in_specs=in_specs, out_specs=out_specs, check_vma=False
    )
```

profile of v0, /device:TPU:0, one launch (start us, length us, event | category | flops | bytes accessed | tf_op | source)
XLA Modules:
  0.0 489.1 jit_solution(2284740775558172705)
XLA Ops:
  7.2 0.7 all-gather.5.cloned.1.call-update
  7.9 0.7 all-gather.3.cloned.1.call-update
  8.7 68.4 %all-gather.5.cloned.1.call-done = bf16[6144,512]{1,0:T(8,128)(2,1)} async-done(((bf16[768,512]{1,0:T(8,128)(2,1)}), bf16[6144,512]{1,0:T(8,128)(2,1)}) %all-gather.5.cloned.1.call-update) | async-done | bytes 6291472 | tf_op jit(solution)/shard_map/all_gather | solution.py:29
  77.1 26.8 %fusion.67 = f32[3072,512]{1,0:T(8,128)} fusion(bf16[3072,6144]{1,0:T(8,128)(2,1)} %bitcast.70, bf16[6144,512]{1,0:T(8,128)(2,1)} %all-gather.5.cloned.1.call-done), kind=kOutput, calls=%fused_computation.91 | convolution fusion | flops 19327352832 | bytes 50331648 | tf_op jit(solution)/shard_map/dot_general | solution.py:41
  103.9 17.5 %all-gather.3.cloned.1.call-done = bf16[3072,512]{1,0:T(8,128)(2,1)} async-done(((bf16[768,512]{1,0:T(8,128)(2,1)}), bf16[3072,512]{1,0:T(8,128)(2,1)}) %all-gather.3.cloned.1.call-update) | async-done | bytes 3145744 | tf_op jit(solution)/shard_map/all_gather | solution.py:28
  121.4 27.7 %fusion.66 = f32[6144,512]{1,0:T(8,128)} fusion(bf16[3072,6144]{1,0:T(8,128)(2,1)} %bitcast.71, bf16[3072,512]{1,0:T(8,128)(2,1)} %all-gather.3.cloned.1.call-done), kind=kOutput, calls=%fused_computation.90 | convolution fusion | flops 19327352832 | bytes 53477376 | tf_op jit(solution)/shard_map/dot_general | solution.py:32
  149.2 1.1 copy-done.6
  150.5 8.0 %while.5 = (s32[]{:T(128)}, f32[512,512]{1,0:T(8,128)S(1)}, s32[4,2]{0,1:T(2,128)S(1)}, f32[4,128,128]{2,1,0:T(8,128)S(1)}, s32[]{:T(128)}) while((s32[]{:T(128)}, f32[512,512]{1,0:T(8,128)S(1)}, s32[4,2]{0,1:T(2,128)S(1)}, f32[4,128,128]{2,1,0:T(8,128)S(1)}, s32[]{:T(128)}) %tuple.32), condition=%wide.while_cond.1, body=%wide.while_body.1.sunk | while | flops 2 | bytes 131181 | solution.py:47
  151.1 1.4 bitcast_dynamic-update-slice_fusion.2
  152.6 0.5 fusion.86
  153.1 1.3 bitcast_dynamic-update-slice_fusion.2
  155.1 1.3 bitcast_dynamic-update-slice_fusion.2
  156.5 0.5 fusion.86
  157.1 1.3 bitcast_dynamic-update-slice_fusion.2
  158.5 39.5 %custom-call.7 = f32[4,128,128]{1,2,0:T(8,128)S(1)} custom-call(f32[4,128,128]{2,1,0:T(8,128)S(1)} %get-tuple-element.18), custom_call_target="InvertDiagBlocksLowerTriangular" | custom-call | tf_op jit(solution)/shard_map/jit(_solve_triangular)/triangular_solve | solution.py:47
  198.0 127.9 %reduce-scatter.3.cloned.1.call-done = f32[768,512]{1,0:T(8,128)} async-done(((f32[6144,512]{1,0:T(8,128)}), f32[768,512]{1,0:T(8,128)}) %reduce-scatter.3.cloned.1.call-update) | async-done | bytes 1572880 | tf_op jit(solution)/shard_map/reduce_scatter | solution.py:31
  325.9 2.9 subtract_bitcast_fusion
  329.3 0.8 convolution_subtract_fusion.1
  330.6 1.4 convolution_subtract_fusion.2
  332.5 2.1 convolution_subtract_fusion
  334.7 1.2 fusion.47
  335.9 3.4 fusion.10
  339.3 1.2 fusion.11
  340.5 1.6 copy.8
  342.2 126.4 %all-reduce.2.cloned.1.call-done = f32[512,512]{1,0:T(8,128)} async-done(((f32[512,512]{1,0:T(8,128)}), f32[512,512]{1,0:T(8,128)}) %all-reduce.2.cloned.1.call-update) | async-done | bytes 1048592 | tf_op jit(solution)/shard_map/psum | solution.py:54
  468.6 3.7 convolution_multiply_fusion
  474.3 0.9 convolution_subtract_fusion.8
  476.1 0.6 convolution_subtract_fusion.4
  477.1 1.0 convolution_subtract_fusion.3
  478.5 1.5 convolution_subtract_fusion.7
  480.8 0.6 copy-done.1
  481.4 1.2 add_multiply_fusion
  (47 shorter events, 7.6 us)
Async XLA Ops:
  7.2 69.9 %all-gather.5.cloned.1.call-start = ((), (), s32[]{:S(2)}) async-start(), calls=%async_computation.4 | async-start | bytes 7077888 | tf_op jit(solution)/shard_map/all_gather | solution.py:29
  7.9 113.5 %all-gather.3.cloned.1.call-start = ((), (), s32[]{:S(2)}) async-start(), calls=%async_computation.2 | async-start | bytes 3932160 | tf_op jit(solution)/shard_map/all_gather | solution.py:28
  8.6 189.3 %reduce-scatter.5.cloned.1.call-start = ((), (), s32[]{:S(2)}) async-start(), calls=%async_computation.5 | async-start | bytes 7864320 | tf_op jit(solution)/shard_map/reduce_scatter | solution.py:40
  103.8 222.1 %reduce-scatter.3.cloned.1.call-start = ((), (), s32[]{:S(2)}) async-start(), calls=%async_computation.3 | async-start | bytes 14155776 | tf_op jit(solution)/shard_map/reduce_scatter | solution.py:31
  149.1 1.2 copy-start.6
  149.1 319.4 %all-reduce.2.cloned.1.call-start = ((), (), s32[]{:S(2)}) async-start(), calls=%async_computation.6 | async-start | bytes 2097152 | tf_op jit(solution)/shard_map/psum | solution.py:54
  198.0 136.7 %copy-start.4 = (f32[4,128,128]{1,2,0:T(8,128)}, f32[4,128,128]{1,2,0:T(8,128)S(1)}, u32[]{:S(2)}) copy-start(f32[4,128,128]{1,2,0:T(8,128)S(1)} %custom-call.7) | copy-start | bytes 786436
  332.5 3.4 copy-start.2
  332.5 3.4 copy-start.3
  342.2 130.1 %copy-start.5 = (f32[4,128,128]{1,2,0:T(8,128)S(1)}, f32[4,128,128]{1,2,0:T(8,128)}, u32[]{:S(2)}) copy-start(f32[4,128,128]{1,2,0:T(8,128)} %copy-done.4) | copy-start | bytes 786436
  478.4 1.9 copy-start
  480.4 1.0 copy-start.1
Sparse Core Ops, SparseCore 0:
  9.6 67.4 all-gather.4
  78.9 42.4 all-gather.2
  124.4 70.1 reduce-scatter.4
  196.8 129.1 reduce-scatter.2
  339.4 129.0 all-reduce.1
where the time goes:
time: 489 us
  waiting for transfers between devices  342 us (70%)
  matrix products  76.4 us (16%)
  other arithmetic  45.1 us (9%)
  between operations  14.1 us (3%)
  local copies, waits for them, and re-layouts  11.6 us (2%)
    reduce_scatter x1, waiting for transfers between devices, on_device(): lax.psum_scatter(lax.dot_general(block, col_panel, (((0,), (0,)), ((), ()...  128 us
    psum x1, waiting for transfers between devices, on_device(): diag_new = diag_grad - lax.psum(contrib, ('row', 'col'))  126 us
    all_gather x1, waiting for transfers between devices, on_device(): row_panel = lax.all_gather(panel, 'col', axis=0, tiled=True)  68.4 us
    another operation x3, other arithmetic, on_device(): jax.scipy.linalg.solve_triangular(lower, reduced.T, lower=True, trans=1)  39.6 us
    dot_general x1, matrix products, on_device(): lax.dot_general(block, col_panel, (((0,), (0,)), ((), ())), preferred_ele...  27.7 us
    dot_general x1, matrix products, on_device(): jnp.dot(block, row_panel, preferred_element_type=jnp.float32)  26.8 us
    all_gather x1, waiting for transfers between devices, on_device(): col_panel = lax.all_gather(panel, 'row', axis=0, tiled=True)  17.5 us
  transfers between devices with their start and end apart: 5, of which 4 were waited for; matrix products, arithmetic and copies ran while one was open for 21% of the time, Pallas kernels for 0%

commit v1 on v0

--- a/solution.py
+++ b/solution.py
@@ -51,7 +51,7 @@
         (((0,), (0,)), ((), ())),
         precision=lax.Precision.HIGHEST,
     )
-    diag_new = diag_grad - lax.psum(contrib, ("row", "col"))
+    diag_new = diag_grad - lax.psum(lax.psum(contrib, "col"), "row")
     inner = halve_lower(jnp.dot(lower.T, keep_lower(diag_new), precision=lax.Precision.HIGHEST))
     left = jax.scipy.linalg.solve_triangular(lower, inner, lower=True, trans=1)
     return (panel_adj, right_solve(left, lower))

time: 489 us -> 473 us (0.967)
  waiting for transfers between devices: 342 us -> 325 us
    psum x1 -> x2, waiting for transfers between devices: 126 us -> 109 us  [on_device(): diag_new = diag_grad - lax.psum(lax.psum(contrib, 'col'), 'row')]
  transfers between devices with their start and end apart: 5 -> 6, of which waited for: 4 -> 5; matrix products, arithmetic and copies ran while one was open for 21% -> 22% of each run, Pallas kernels for 0% -> 0%
where the time goes in v1:
time: 473 us; the launch traced here: 472 us
  waiting for transfers between devices  325 us (69%)
  matrix products  76.1 us (16%)
  other arithmetic  44.9 us (9%)
  between operations  14.4 us (3%)
  local copies, waits for them, and re-layouts  11.4 us (2%)
    reduce_scatter x1, waiting for transfers between devices, on_device(): lax.psum_scatter(lax.dot_general(block, col_panel, (((0,), (0,)), ((), ()...  128 us
    psum x2, waiting for transfers between devices, on_device(): diag_new = diag_grad - lax.psum(lax.psum(contrib, 'col'), 'row')  109 us
    all_gather x1, waiting for transfers between devices, on_device(): row_panel = lax.all_gather(panel, 'col', axis=0, tiled=True)  68.4 us
    another operation x3, other arithmetic, on_device(): jax.scipy.linalg.solve_triangular(lower, reduced.T, lower=True, trans=1)  39.4 us
    dot_general x1, matrix products, on_device(): lax.dot_general(block, col_panel, (((0,), (0,)), ((), ())), preferred_ele...  27.7 us
    dot_general x1, matrix products, on_device(): jnp.dot(block, row_panel, preferred_element_type=jnp.float32)  26.8 us
    all_gather x1, waiting for transfers between devices, on_device(): col_panel = lax.all_gather(panel, 'row', axis=0, tiled=True)  17.5 us
  transfers between devices with their start and end apart: 6, of which 5 were waited for; matrix products, arithmetic and copies ran while one was open for 22% of the time, Pallas kernels for 0%

profile of v1, /device:TPU:0, one launch (start us, length us, event | category | flops | bytes accessed | tf_op | source)
XLA Modules:
  0.0 472.3 jit_solution(14553033127311113500)
XLA Ops:
  7.2 0.7 all-gather.5.cloned.1.call-update
  7.9 0.7 all-gather.3.cloned.1.call-update
  8.7 68.4 %all-gather.5.cloned.1.call-done = bf16[6144,512]{1,0:T(8,128)(2,1)} async-done(((bf16[768,512]{1,0:T(8,128)(2,1)}), bf16[6144,512]{1,0:T(8,128)(2,1)}) %all-gather.5.cloned.1.call-update) | async-done | bytes 6291472 | tf_op jit(solution)/shard_map/all_gather | solution.py:29
  77.1 26.8 %fusion.67 = f32[3072,512]{1,0:T(8,128)} fusion(bf16[3072,6144]{1,0:T(8,128)(2,1)} %bitcast.70, bf16[6144,512]{1,0:T(8,128)(2,1)} %all-gather.5.cloned.1.call-done), kind=kOutput, calls=%fused_computation.91 | convolution fusion | flops 19327352832 | bytes 50331648 | tf_op jit(solution)/shard_map/dot_general | solution.py:41
  103.9 17.5 %all-gather.3.cloned.1.call-done = bf16[3072,512]{1,0:T(8,128)(2,1)} async-done(((bf16[768,512]{1,0:T(8,128)(2,1)}), bf16[3072,512]{1,0:T(8,128)(2,1)}) %all-gather.3.cloned.1.call-update) | async-done | bytes 3145744 | tf_op jit(solution)/shard_map/all_gather | solution.py:28
  121.4 27.7 %fusion.66 = f32[6144,512]{1,0:T(8,128)} fusion(bf16[3072,6144]{1,0:T(8,128)(2,1)} %bitcast.71, bf16[3072,512]{1,0:T(8,128)(2,1)} %all-gather.3.cloned.1.call-done), kind=kOutput, calls=%fused_computation.90 | convolution fusion | flops 19327352832 | bytes 53477376 | tf_op jit(solution)/shard_map/dot_general | solution.py:32
  149.4 0.9 copy-done.6
  150.5 8.0 %while.5 = (s32[]{:T(128)}, f32[512,512]{1,0:T(8,128)S(1)}, s32[4,2]{0,1:T(2,128)S(1)}, f32[4,128,128]{2,1,0:T(8,128)S(1)}, s32[]{:T(128)}) while((s32[]{:T(128)}, f32[512,512]{1,0:T(8,128)S(1)}, s32[4,2]{0,1:T(2,128)S(1)}, f32[4,128,128]{2,1,0:T(8,128)S(1)}, s32[]{:T(128)}) %tuple.32), condition=%wide.while_cond.1, body=%wide.while_body.1.sunk | while | flops 2 | bytes 131181 | solution.py:47
  151.1 1.4 bitcast_dynamic-update-slice_fusion.2
  152.6 0.5 fusion.86
  153.1 1.3 bitcast_dynamic-update-slice_fusion.2
  155.1 1.3 bitcast_dynamic-update-slice_fusion.2
  157.1 1.3 bitcast_dynamic-update-slice_fusion.2
  158.5 39.3 %custom-call.7 = f32[4,128,128]{1,2,0:T(8,128)S(1)} custom-call(f32[4,128,128]{2,1,0:T(8,128)S(1)} %get-tuple-element.18), custom_call_target="InvertDiagBlocksLowerTriangular" | custom-call | tf_op jit(solution)/shard_map/jit(_solve_triangular)/triangular_solve | solution.py:47
  197.8 128.1 %reduce-scatter.3.cloned.1.call-done = f32[768,512]{1,0:T(8,128)} async-done(((f32[6144,512]{1,0:T(8,128)}), f32[768,512]{1,0:T(8,128)}) %reduce-scatter.3.cloned.1.call-update) | async-done | bytes 1572880 | tf_op jit(solution)/shard_map/reduce_scatter | solution.py:31
  325.9 2.9 subtract_bitcast_fusion
  329.3 0.8 convolution_subtract_fusion.1
  330.6 1.4 convolution_subtract_fusion.2
  332.5 2.1 convolution_subtract_fusion
  334.7 1.2 fusion.47
  335.9 3.4 fusion.10
  339.6 57.7 %all-reduce.3.cloned.1.call-done = f32[512,512]{1,0:T(8,128)} async-done(((f32[512,512]{1,0:T(8,128)}), f32[512,512]{1,0:T(8,128)}) %all-reduce.3.cloned.1.call-update) | async-done | bytes 1048592 | tf_op jit(solution)/shard_map/psum | solution.py:54
  397.3 1.2 fusion.11
  398.5 1.6 copy.8
  400.1 51.6 %all-reduce.5.cloned.1.call-done = f32[512,512]{1,0:T(8,128)} async-done(((f32[512,512]{1,0:T(8,128)}), f32[512,512]{1,0:T(8,128)}) %all-reduce.5.cloned.1.call-update) | async-done | bytes 1048592 | tf_op jit(solution)/shard_map/psum | solution.py:54
  451.8 3.7 convolution_multiply_fusion
  457.5 0.7 convolution_subtract_fusion.8
  459.0 0.6 convolution_subtract_fusion.4
  460.0 1.0 convolution_subtract_fusion.3
  461.4 1.5 convolution_subtract_fusion.7
  463.7 0.6 copy-done.1
  464.3 1.2 add_multiply_fusion
  (50 shorter events, 8.6 us)
Async XLA Ops:
  7.2 69.9 %all-gather.5.cloned.1.call-start = ((), (), s32[]{:S(2)}) async-start(), calls=%async_computation.4 | async-start | bytes 7077888 | tf_op jit(solution)/shard_map/all_gather | solution.py:29
  7.9 113.5 %all-gather.3.cloned.1.call-start = ((), (), s32[]{:S(2)}) async-start(), calls=%async_computation.2 | async-start | bytes 3932160 | tf_op jit(solution)/shard_map/all_gather | solution.py:28
  8.6 189.2 %reduce-scatter.5.cloned.1.call-start = ((), (), s32[]{:S(2)}) async-start(), calls=%async_computation.5 | async-start | bytes 7864320 | tf_op jit(solution)/shard_map/reduce_scatter | solution.py:40
  103.8 222.1 %reduce-scatter.3.cloned.1.call-start = ((), (), s32[]{:S(2)}) async-start(), calls=%async_computation.3 | async-start | bytes 14155776 | tf_op jit(solution)/shard_map/reduce_scatter | solution.py:31
  149.1 1.2 copy-start.6
  149.1 248.1 %all-reduce.3.cloned.1.call-start = ((), (), s32[]{:S(2)}) async-start(), calls=%async_computation.6 | async-start | bytes 2097152 | tf_op jit(solution)/shard_map/psum | solution.py:54
  197.8 136.9 %copy-start.4 = (f32[4,128,128]{1,2,0:T(8,128)}, f32[4,128,128]{1,2,0:T(8,128)S(1)}, u32[]{:S(2)}) copy-start(f32[4,128,128]{1,2,0:T(8,128)S(1)} %custom-call.7) | copy-start | bytes 786436
  332.5 3.4 copy-start.2
  332.5 3.4 copy-start.3
  339.3 112.5 %all-reduce.5.cloned.1.call-start = ((), (), s32[]{:S(2)}) async-start(), calls=%async_computation.7 | async-start | bytes 2097152 | tf_op jit(solution)/shard_map/psum | solution.py:54
  400.1 55.4 %copy-start.5 = (f32[4,128,128]{1,2,0:T(8,128)S(1)}, f32[4,128,128]{1,2,0:T(8,128)}, u32[]{:S(2)}) copy-start(f32[4,128,128]{1,2,0:T(8,128)} %copy-done.4) | copy-start | bytes 786436
  461.4 1.9 copy-start
  463.4 1.0 copy-start.1
Sparse Core Ops, SparseCore 0:
  9.6 67.4 all-gather.4
  78.9 42.4 all-gather.2
  124.4 70.1 reduce-scatter.4
  196.8 129.1 reduce-scatter.2
  339.4 57.7 all-reduce.2
  400.2 51.5 all-reduce.4
